TPU v7x, 32 devices: a whole 2x2x4 slice. The times are simulated.
32 devices in a mesh: expert: 8 (over z, core), tensor: 4 (over y, x).
Axes of the slice: x: 2, y: 2, z: 4, core: 2. Of those that a mesh axis runs over, the one named last changes fastest.
Arguments:
- tokens: bfloat16 [256, 4096], P('expert', 'tensor'), may hold values from -6 to 6
- cotangent: bfloat16 [256, 4096], P('expert', 'tensor'), may hold values from -6 to 6
- expert_ids: int32 [256, 8], P('expert'), may hold values from 0 to 63, all different within a row; in each aligned block of 32 rows (0 to 31, 32 to 63, ...) at most 8 rows name the same one
- route_weight: float32 [256, 8], P('expert'), may hold values from 0.05 to 0.25
- w_gate: bfloat16 [64, 4096, 1536], P('expert', 'tensor'), may hold values from -0.09375 to 0.09375
- w_up: bfloat16 [64, 4096, 1536], P('expert', 'tensor'), may hold values from -0.09375 to 0.09375
- w_down: bfloat16 [64, 1536, 4096], P('expert', None, 'tensor'), may hold values from -0.15625 to 0.15625
Outputs:
- mixed_out: bfloat16 [256, 4096], P('expert', 'tensor')
- input_grad: bfloat16 [256, 4096], P('expert', 'tensor')
- down_grad: bfloat16 [64, 1536, 4096], P('expert', None, 'tensor')
Inputs may be any that keep to these rules, and one draw needn't show every extreme that they name: `expert_ids`: each row names 8 different experts; within the 32 rows of one device no expert is named more than 8 times.
All inputs are finite; a program needn't handle non-finite values.
Results may differ from a plain program's by a relative error of at most 0.023.
Values may be sent and summed in bfloat16 or wider, within the bound.
No kernel may reach another device: no remote copies, remote signals or barrier semaphores. Data moves between devices by JAX's collectives and lax.ppermute only.
A program may use at most 192 MiB of HBM per device.

v0:
```python
import jax
import jax.numpy as jnp
from jax import lax
from jax.sharding import PartitionSpec as P


def local(tokens, cotangent, expert_ids, route_weight, w_gate, w_up, w_down):
    resident_specialists = w_gate.shape[0]
    experts = resident_specialists * lax.axis_size("expert")
    tok_count = expert_ids.shape[0]
    top_count = expert_ids.shape[1]
    capacity = 2 * tok_count * top_count // experts
    model_width = tokens.shape[1]
    flat_ids = expert_ids.reshape(-1)
    onehot = (flat_ids[:, None] == jnp.arange(experts, dtype=jnp.int32)[None, :]).astype(jnp.int32)
    before = jnp.cumsum(onehot, axis=0) - onehot
    slot_index = jnp.sum(before * onehot, axis=1)
    target = flat_ids * capacity + slot_index
    chosen = (target[:, None] == jnp.arange(experts * capacity, dtype=jnp.int32)[None, :]).astype(
        jnp.float32
    )
    chosen = chosen.reshape(tok_count, top_count, experts * capacity)
    expert_assignment = jnp.sum(chosen, axis=1)
    weighted = jnp.sum(chosen * route_weight[:, :, None], axis=1)
    token_send = jnp.dot(
        expert_assignment.T.astype(jnp.bfloat16), tokens, preferred_element_type=jnp.float32
    )
    token_send = token_send.astype(jnp.bfloat16).reshape(experts, capacity, model_width)
    gradient_outgoing = jnp.dot(
        weighted.T, cotangent, precision=lax.Precision.HIGHEST, preferred_element_type=jnp.float32
    )
    gradient_outgoing = gradient_outgoing.astype(jnp.bfloat16).reshape(
        experts, capacity, model_width
    )
    token_rows, grad_rows = (
        lax.all_to_all(token_send, "expert", split_axis=0, concat_axis=1, tiled=True),
        lax.all_to_all(gradient_outgoing, "expert", split_axis=0, concat_axis=1, tiled=True),
    )
    pre_gate = jnp.einsum("erd,edf->erf", token_rows, w_gate, preferred_element_type=jnp.float32)
    pre_up = jnp.einsum("erd,edf->erf", token_rows, w_up, preferred_element_type=jnp.float32)
    slice_breadth = w_gate.shape[2] // lax.axis_size("tensor")
    gate_sum, up_sum = (
        lax.psum(pre_gate.astype(jnp.bfloat16), "tensor").astype(jnp.float32),
        lax.psum(pre_up.astype(jnp.bfloat16), "tensor").astype(jnp.float32),
    )
    sigmoid_all = jax.nn.sigmoid(gate_sum)
    hidden = (gate_sum * sigmoid_all * up_sum).astype(jnp.bfloat16)
    out_rows = jnp.einsum(
        "erf,efd->erd", hidden, w_down, preferred_element_type=jnp.float32
    ).astype(jnp.bfloat16)
    down_grad = jnp.einsum("erf,erd->efd", hidden, grad_rows, preferred_element_type=jnp.float32)
    offset = lax.axis_index("tensor") * slice_breadth
    gate_part = lax.dynamic_slice_in_dim(gate_sum, offset, slice_breadth, 2)
    up_part = lax.dynamic_slice_in_dim(up_sum, offset, slice_breadth, 2)
    sigmoid_part = lax.dynamic_slice_in_dim(sigmoid_all, offset, slice_breadth, 2)
    hidden_term = jnp.einsum("erd,efd->erf", grad_rows, w_down, preferred_element_type=jnp.float32)
    hidden_grad = lax.psum_scatter(
        hidden_term.astype(jnp.bfloat16), "tensor", scatter_dimension=2, tiled=True
    ).astype(jnp.float32)
    gate_grad = (
        hidden_grad * up_part * sigmoid_part * (1.0 + gate_part * (1.0 - sigmoid_part))
    ).astype(jnp.bfloat16)
    up_grad = (hidden_grad * gate_part * sigmoid_part).astype(jnp.bfloat16)
    gate_piece = lax.all_gather(gate_grad, "tensor", axis=2, tiled=True)
    up_piece = lax.all_gather(up_grad, "tensor", axis=2, tiled=True)
    running = jnp.einsum("erf,edf->erd", gate_piece, w_gate, preferred_element_type=jnp.float32)
    input_rows = running + jnp.einsum(
        "erf,edf->erd", up_piece, w_up, preferred_element_type=jnp.float32
    )
    input_rows = input_rows.astype(jnp.bfloat16)
    returned_out, returned_in = (
        lax.all_to_all(out_rows, "expert", split_axis=1, concat_axis=0, tiled=True),
        lax.all_to_all(input_rows, "expert", split_axis=1, concat_axis=0, tiled=True),
    )
    returned_out = returned_out.reshape(experts * capacity, model_width)
    returned_in = returned_in.reshape(experts * capacity, model_width)
    mixed_out = jnp.dot(
        weighted, returned_out, precision=lax.Precision.HIGHEST, preferred_element_type=jnp.float32
    )
    input_grad = jnp.dot(
        expert_assignment.astype(jnp.bfloat16), returned_in, preferred_element_type=jnp.float32
    )
    return (
        mixed_out.astype(jnp.bfloat16),
        input_grad.astype(jnp.bfloat16),
        down_grad.astype(jnp.bfloat16),
    )


def solution(mesh):
    return jax.shard_map(
        local,
        mesh=mesh,
        in_specs=(
            P("expert", "tensor"),
            P("expert", "tensor"),
            P("expert", None),
            P("expert", None),
            P("expert", "tensor", None),
            P("expert", "tensor", None),
            P("expert", None, "tensor"),
        ),
        out_specs=(P("expert", "tensor"), P("expert", "tensor"), P("expert", None, "tensor")),
        check_vma=False,
    )
```

profile of v0, /device:TPU:0, one launch (start us, length us, event | category | flops | bytes accessed | tf_op | source)
XLA Modules:
  0.0 326.9 jit_solution(5938493697258200641)
XLA Ops:
  7.2 0.0 copy-start
  7.2 0.0 copy-start.6
  7.2 0.8 copy.45
  8.0 0.1 eq.43
  8.1 0.1 eq.39
  8.2 0.8 copy.49
  8.9 0.6 reduce-window.6
  9.6 0.2 slice_reduce_fusion
  9.8 0.1 fusion.17
  9.9 0.1 reduce_sum.30
  10.0 0.4 convert_reduce_fusion
  10.4 0.0 copy-start.4
  10.4 0.6 copy-done.4
  11.0 0.0 copy-done
  11.0 1.4 fusion
  12.4 6.4 %all-to-all-start = ((bf16[64,8,1024]{2,1,0:T(8,128)(2,1)}), bf16[64,8,1024]{2,1,0:T(8,128)(2,1)S(1)}, u32[]{:S(2)}, u32[]{:S(2)}) async-start(bf16[64,8,1024]{2,1,0:T(8,128)(2,1)} %fusion), calls=%async_computation | async-start | bytes 2097152 | tf_op jit(solution)/shard_map/all_to_all | solution.py:36
  18.8 0.0 copy-done.6
  18.8 2.0 fusion.1
  20.8 24.5 %all-to-all-done = bf16[64,8,1024]{2,1,0:T(8,128)(2,1)S(1)} async-done(((bf16[64,8,1024]{2,1,0:T(8,128)(2,1)}), bf16[64,8,1024]{2,1,0:T(8,128)(2,1)S(1)}, u32[]{:S(2)}, u32[]{:S(2)}) %all-to-all-start) | async-done | bytes 1048608 | tf_op jit(solution)/shard_map/all_to_all | solution.py:36
  45.4 3.6 %all-to-all-start.2 = ((bf16[64,8,1024]{2,1,0:T(8,128)(2,1)}), bf16[64,8,1024]{2,1,0:T(8,128)(2,1)S(1)}, u32[]{:S(2)}, u32[]{:S(2)}) async-start(bf16[64,8,1024]{2,1,0:T(8,128)(2,1)} %fusion.1), calls=%async_computation.2 | async-start | bytes 2097152 | tf_op jit(solution)/shard_map/all_to_all | solution.py:37
  48.9 0.0 all-reduce.3.cloned.1.call-start
  49.0 13.7 %convolution_convert_fusion.2 = bf16[8,64,1536]{2,1,0:T(8,128)(2,1)} fusion(bf16[8,1024,1536]{2,1,0:T(8,128)(2,1)} %param.12, bf16[8,8,8,1024]{3,2,1,0:T(8,128)(2,1)S(1)} %bitcast.68), kind=kOutput, calls=%fused_computation.4 | convolution fusion | flops 1611399168 | bytes 27787264 | tf_op jit(solution)/shard_map/erd,edf->erf/dot_general | solution.py:40
  62.7 13.7 %convolution_convert_fusion.3 = bf16[8,64,1536]{2,1,0:T(8,128)(2,1)} fusion(bf16[8,1024,1536]{2,1,0:T(8,128)(2,1)} %param.11, bf16[8,8,8,1024]{3,2,1,0:T(8,128)(2,1)S(1)} %bitcast.69), kind=kOutput, calls=%fused_computation.5 | convolution fusion | flops 1611399168 | bytes 27787264 | tf_op jit(solution)/shard_map/erd,edf->erf/dot_general | solution.py:39
  76.4 0.0 all-reduce.3.cloned.1.call-update
  76.4 0.0 reduce-scatter.4.cloned.1.call-start
  76.5 0.0 all-to-all-done.2
  76.5 13.2 %convolution_convert_fusion.1 = bf16[8,64,1536]{2,1,0:T(8,128)(2,1)S(1)} fusion(bf16[8,1536,1024]{2,1,0:T(8,128)(2,1)} %param.13, bf16[8,8,8,1024]{3,2,1,0:T(8,128)(2,1)S(1)} %bitcast.65), kind=kOutput, calls=%fused_computation.3 | convolution fusion | flops 1611399168 | bytes 27787264 | tf_op jit(solution)/shard_map/erd,efd->erf/dot_general | solution.py:56
  89.7 3.5 %copy.60 = bf16[8,64,1536]{1,0,2:T(8,128)(2,1)} copy(bf16[8,64,1536]{2,1,0:T(8,128)(2,1)S(1)} %convolution_convert_fusion.1) | data formatting | bytes 3145728
  93.2 5.4 %reshape.61 = bf16[1536,512]{1,0:T(8,128)(2,1)} reshape(bf16[1536,8,64]{2,1,0:T(8,128)(2,1)} %bitcast.67) | data formatting | bytes 3145728
  98.6 0.0 reduce-scatter.4.cloned.1.call-update
  98.6 0.2 all-gather.3.cloned.1.call-start
  98.9 66.0 %all-reduce.3.cloned.1.call-done = (bf16[8,64,1536]{2,1,0:T(8,128)(2,1)}, bf16[8,64,1536]{2,1,0:T(8,128)(2,1)}) async-done(((bf16[8,64,1536]{2,1,0:T(8,128)(2,1)}, bf16[8,64,1536]{2,1,0:T(8,128)(2,1)}), (bf16[8,64,1536]{2,1,0:T(8,128)(2,1)}, bf16[8,64,1536]{2,1,0:T(8,128)(2,1)})) %all-reduce.3.cloned.1.call-update) | async-done | bytes 3145744 | tf_op jit(solution)/shard_map/psum | solution.py:43
  164.9 0.0 copy-start.2
  164.9 3.6 %convert_element_type.70 = f32[8,64,1536]{2,1,0:T(8,128)} convert(bf16[8,64,1536]{2,1,0:T(8,128)(2,1)} %get-tuple-element.5) | non-fusion elementwise | flops 786432 | bytes 4718592 | tf_op jit(solution)/shard_map/convert_element_type | solution.py:43
  168.5 0.0 copy-done.2
  168.5 2.5 add_divide_fusion
  171.0 28.1 %reduce-scatter.4.cloned.1.call-done = bf16[384,512]{1,0:T(8,128)(2,1)} async-done(((bf16[1536,512]{1,0:T(8,128)(2,1)}), bf16[384,512]{1,0:T(8,128)(2,1)}) %reduce-scatter.4.cloned.1.call-update) | async-done | bytes 393232
  199.0 1.5 reshape.62
  200.6 1.3 copy.61
  201.8 0.0 copy-start.3
  201.8 1.8 convert_element_type.72
  203.7 0.0 copy-done.3
  203.7 2.6 fusion.14
  206.3 0.0 all-gather.3.cloned.1.call-update
  206.3 0.0 all-gather.5.cloned.1.call-start
  206.4 0.5 all-gather.5.cloned.1.call-update
  206.9 13.5 %convolution_convert_fusion.4 = bf16[8,64,1024]{2,1,0:T(8,128)(2,1)S(1)} fusion(bf16[8,1536,1024]{2,1,0:T(8,128)(2,1)} %param.13, bf16[8,64,1536]{2,1,0:T(8,128)(2,1)S(1)} %copy-done.2, bf16[8,64,1536]{2,1,0:T(8,128)(2,1)} %get-tuple-element.6), kind=kOutput, calls=%fused_computation.7 | convolution fusion | flops 1617428480 | bytes 29360128 | tf_op jit(solution)/shard_map/erf,efd->erd/dot_general | solution.py:48
  220.4 1.6 copy.51
  222.0 4.6 %all-to-all-start.1 = ((bf16[8,64,1024]{2,0,1:T(8,128)(2,1)}), bf16[8,64,1024]{2,0,1:T(8,128)(2,1)}, u32[]{:S(2)}, u32[]{:S(2)}) async-start(bf16[8,64,1024]{2,0,1:T(8,128)(2,1)} %copy.51), calls=%async_computation.1 | async-start | bytes 2097152 | tf_op jit(solution)/shard_map/all_to_all | solution.py:72
  226.6 10.6 %all-gather.3.cloned.1.call-done = bf16[8,64,1536]{2,1,0:T(8,128)(2,1)} async-done(((bf16[8,64,384]{2,1,0:T(8,128)(2,1)}), bf16[8,64,1536]{2,1,0:T(8,128)(2,1)}) %all-gather.3.cloned.1.call-update) | async-done | bytes 1572880 | tf_op jit(solution)/shard_map/all_gather | solution.py:64
  237.2 13.8 %fusion.21 = f32[8,64,1024]{2,1,0:T(8,128)} fusion(bf16[8,64,1536]{2,1,0:T(8,128)(2,1)} %all-gather.3.cloned.1.call-done, bf16[8,1024,1536]{2,1,0:T(8,128)(2,1)} %param.11), kind=kOutput, calls=%fused_computation.44 | convolution fusion | flops 1610612736 | bytes 28835840 | tf_op jit(solution)/shard_map/erf,edf->erd/dot_general | solution.py:66
  251.0 18.6 %all-gather.5.cloned.1.call-done = bf16[8,64,1536]{2,1,0:T(8,128)(2,1)} async-done(((bf16[8,64,384]{2,1,0:T(8,128)(2,1)}), bf16[8,64,1536]{2,1,0:T(8,128)(2,1)}) %all-gather.5.cloned.1.call-update) | async-done | bytes 1572880 | tf_op jit(solution)/shard_map/all_gather | solution.py:65
  269.6 14.0 %add_convert_fusion = bf16[8,64,1024]{2,1,0:T(8,128)(2,1)} fusion(f32[8,64,1024]{2,1,0:T(8,128)} %fusion.21, bf16[8,64,1536]{2,1,0:T(8,128)(2,1)} %all-gather.5.cloned.1.call-done, bf16[8,1024,1536]{2,1,0:T(8,128)(2,1)} %param.12), kind=kOutput, calls=%fused_computation.6 | convolution fusion | flops 1611661312 | bytes 29884416 | tf_op jit(solution)/shard_map/erf,edf->erd/dot_general | solution.py:67
  283.6 2.8 copy.55
  286.3 0.0 all-to-all-done.1
  286.3 4.6 %all-to-all-start.3 = ((bf16[8,64,1024]{2,0,1:T(8,128)(2,1)}), bf16[8,64,1024]{2,0,1:T(8,128)(2,1)}, u32[]{:S(2)}, u32[]{:S(2)}) async-start(bf16[8,64,1024]{2,0,1:T(8,128)(2,1)} %copy.55), calls=%async_computation.3 | async-start | bytes 2097152 | tf_op jit(solution)/shard_map/all_to_all | solution.py:73
  291.0 13.8 %convolution_convert_fusion = bf16[8,1536,1024]{2,1,0:T(8,128)(2,1)} fusion(bf16[8,8,8,1024]{3,2,1,0:T(8,128)(2,1)S(1)} %bitcast.66, bf16[8,64,1536]{2,1,0:T(8,128)(2,1)S(1)} %copy-done.2, bf16[8,64,1536]{2,1,0:T(8,128)(2,1)} %get-tuple-element.6), kind=kOutput, calls=%fused_computation | convolution fusion | flops 1629487104 | bytes 29360128 | tf_op jit(solution)/shard_map/erf,erd->efd/dot_general | solution.py:51
  304.8 1.9 copy.53
  306.6 1.2 convolution_convert_fusion.8
  307.9 9.8 %all-to-all-done.3 = bf16[8,64,1024]{2,0,1:T(8,128)(2,1)} async-done(((bf16[8,64,1024]{2,0,1:T(8,128)(2,1)}), bf16[8,64,1024]{2,0,1:T(8,128)(2,1)}, u32[]{:S(2)}, u32[]{:S(2)}) %all-to-all-start.3) | async-done | bytes 1048608 | tf_op jit(solution)/shard_map/all_to_all | solution.py:73
  317.6 1.8 copy.57
  319.4 0.0 copy-done.5
  319.5 0.9 convolution_convert_fusion.7
  320.4 0.0 copy-done.1
  (6 shorter events, 0.1 us)
Async XLA Ops:
  7.2 3.9 %copy-start = (bf16[32,1024]{1,0:T(8,128)(2,1)S(1)}, bf16[32,1024]{1,0:T(8,128)(2,1)}, u32[]{:S(2)}) copy-start(bf16[32,1024]{1,0:T(8,128)(2,1)} %param.7) | copy-start | bytes 196612
  7.2 11.6 %copy-start.6 = (bf16[32,1024]{1,0:T(8,128)(2,1)S(1)}, bf16[32,1024]{1,0:T(8,128)(2,1)}, u32[]{:S(2)}) copy-start(bf16[32,1024]{1,0:T(8,128)(2,1)} %param.8) | copy-start | bytes 196612
  10.4 0.6 copy-start.4
  12.4 32.9 %all-to-all-start = ((bf16[64,8,1024]{2,1,0:T(8,128)(2,1)}), bf16[64,8,1024]{2,1,0:T(8,128)(2,1)S(1)}, u32[]{:S(2)}, u32[]{:S(2)}) async-start(bf16[64,8,1024]{2,1,0:T(8,128)(2,1)} %fusion), calls=%async_computation | async-start | bytes 2097152 | tf_op jit(solution)/shard_map/all_to_all | solution.py:36
  45.4 31.1 %all-to-all-start.2 = ((bf16[64,8,1024]{2,1,0:T(8,128)(2,1)}), bf16[64,8,1024]{2,1,0:T(8,128)(2,1)S(1)}, u32[]{:S(2)}, u32[]{:S(2)}) async-start(bf16[64,8,1024]{2,1,0:T(8,128)(2,1)} %fusion.1), calls=%async_computation.2 | async-start | bytes 2097152 | tf_op jit(solution)/shard_map/all_to_all | solution.py:37
  48.9 116.0 %all-reduce.3.cloned.1.call-start = ((), (), s32[]{:S(2)}) async-start(), calls=%async_computation.8 | async-start | bytes 6291456 | tf_op jit(solution)/shard_map/psum | solution.py:43
  76.4 122.6 %reduce-scatter.4.cloned.1.call-start = ((), (), s32[]{:S(2)}) async-start(), calls=%async_computation.7 | async-start | bytes 1966080
  98.6 138.5 %all-gather.3.cloned.1.call-start = ((), (), s32[]{:S(2)}) async-start(), calls=%async_computation.5 | async-start | bytes 1966080 | tf_op jit(solution)/shard_map/all_gather | solution.py:64
  164.9 3.6 %copy-start.2 = (bf16[8,64,1536]{2,1,0:T(8,128)(2,1)S(1)}, bf16[8,64,1536]{2,1,0:T(8,128)(2,1)}, u32[]{:S(2)}) copy-start(bf16[8,64,1536]{2,1,0:T(8,128)(2,1)} %get-tuple-element.5) | copy-start | bytes 4718596
  201.8 1.9 copy-start.3
  206.3 63.3 %all-gather.5.cloned.1.call-start = ((), (), s32[]{:S(2)}) async-start(), calls=%async_computation.6 | async-start | bytes 1966080 | tf_op jit(solution)/shard_map/all_gather | solution.py:65
  222.0 64.3 %all-to-all-start.1 = ((bf16[8,64,1024]{2,0,1:T(8,128)(2,1)}), bf16[8,64,1024]{2,0,1:T(8,128)(2,1)}, u32[]{:S(2)}, u32[]{:S(2)}) async-start(bf16[8,64,1024]{2,0,1:T(8,128)(2,1)} %copy.51), calls=%async_computation.1 | async-start | bytes 2097152 | tf_op jit(solution)/shard_map/all_to_all | solution.py:72
  286.3 31.3 %all-to-all-start.3 = ((bf16[8,64,1024]{2,0,1:T(8,128)(2,1)}), bf16[8,64,1024]{2,0,1:T(8,128)(2,1)}, u32[]{:S(2)}, u32[]{:S(2)}) async-start(bf16[8,64,1024]{2,0,1:T(8,128)(2,1)} %copy.55), calls=%async_computation.3 | async-start | bytes 2097152 | tf_op jit(solution)/shard_map/all_to_all | solution.py:73
  304.8 14.7 %copy-start.5 = (bf16[32,512]{1,0:T(8,128)(2,1)S(1)}, bf16[32,512]{1,0:T(8,128)(2,1)}, u32[]{:S(2)}) copy-start(bf16[32,512]{1,0:T(8,128)(2,1)} %copy-done.4) | copy-start | bytes 98308
  304.8 15.6 %copy-start.1 = (bf16[32,1024]{1,0:T(8,128)(2,1)S(1)}, bf16[32,1024]{1,0:T(8,128)(2,1)}, u32[]{:S(2)}) copy-start(bf16[32,1024]{1,0:T(8,128)(2,1)} %param.7) | copy-start | bytes 196612
Sparse Core Ops, SparseCore 0:
  76.5 88.3 all-reduce.2
  167.9 31.1 reduce-scatter.3
  206.4 30.6 all-gather.2
  238.8 30.6 all-gather.4
where the time goes:
time: 328 us; the launch traced here: 327 us
  waiting for transfers between devices  158 us (48%)
  matrix products  101 us (31%)
  local copies, waits for them, and re-layouts  22.4 us (7%)
  starting transfers between devices  19.4 us (6%)
  between operations  13.9 us (4%)
  other arithmetic  11.7 us (4%)
    psum x1, waiting for transfers between devices, local(): lax.psum(pre_gate.astype(jnp.bfloat16), 'tensor').astype(jnp.float32)  66 us
    unnamed x5, waiting for transfers between devices  28.6 us
    all_to_all x1, waiting for transfers between devices, local(): lax.all_to_all(token_send, 'expert', split_axis=0, concat_axis=1, tiled=T...  24.5 us
    all_gather x1, waiting for transfers between devices, local(): up_piece = lax.all_gather(up_grad, 'tensor', axis=2, tiled=True)  18.6 us
    dot_general x1, matrix products, local(): jnp.einsum('erf,edf->erd', up_piece, w_up, preferred_element_type=jnp.flo...  14 us
    unnamed x20, local copies, waits for them, and re-layouts  13.9 us
    dot_general x1, matrix products, local(): jnp.einsum('erf,erd->efd', hidden, grad_rows, preferred_element_type=jnp....  13.8 us
    dot_general x1, matrix products, local(): jnp.einsum('erf,edf->erd', gate_piece, w_gate, preferred_element_type=jnp...  13.8 us
  transfers between devices with their start and end apart: 8, of which 6 were waited for; matrix products, arithmetic and copies ran while one was open for 37% of the time, Pallas kernels for 0%

commit v1 on v0

--- a/solution.py
+++ b/solution.py
@@ -2,6 +2,18 @@
 import jax.numpy as jnp
 from jax import lax
 from jax.sharding import PartitionSpec as P
+
+
+def product_in_turn(value, axis, dim, term):
+    devices, mine, extent = (lax.axis_size(axis), lax.axis_index(axis), value.shape[dim])
+    ahead = [(i, (i + 1) % devices) for i in range(devices)]
+    carried, total = (value, None)
+    for step in range(devices):
+        coming = lax.ppermute(carried, axis, ahead) if step < devices - 1 else None
+        update = term(carried, (mine - step) % devices * extent)
+        total = update if total is None else total + update
+        carried = coming
+    return total
 
 
 def local(tokens, cotangent, expert_ids, route_weight, w_gate, w_up, w_down):
@@ -62,10 +74,17 @@
     ).astype(jnp.bfloat16)
     up_grad = (hidden_grad * gate_part * sigmoid_part).astype(jnp.bfloat16)
     gate_piece = lax.all_gather(gate_grad, "tensor", axis=2, tiled=True)
-    up_piece = lax.all_gather(up_grad, "tensor", axis=2, tiled=True)
     running = jnp.einsum("erf,edf->erd", gate_piece, w_gate, preferred_element_type=jnp.float32)
-    input_rows = running + jnp.einsum(
-        "erf,edf->erd", up_piece, w_up, preferred_element_type=jnp.float32
+    input_rows = running + product_in_turn(
+        up_grad,
+        "tensor",
+        2,
+        lambda shard, at: jnp.einsum(
+            "erf,edf->erd",
+            shard,
+            lax.dynamic_slice_in_dim(w_up, at, shard.shape[2], axis=2),
+            preferred_element_type=jnp.float32,
+        ),
     )
     input_rows = input_rows.astype(jnp.bfloat16)
     returned_out, returned_in = (

time: 328 us -> 317 us (0.966)
  waiting for transfers between devices: 158 us -> 134 us
  matrix products: 101 us -> 113 us
    all_gather x1 -> x0, waiting for transfers between devices: 18.6 us -> none  [local(): up_piece = lax.all_gather(up_grad, 'tensor', axis=2, tiled=True)]
    dot_general x1 -> x4, matrix products: 14 us -> 26.1 us  [local(): jnp.einsum('erf,edf->erd', shard, lax.dynamic_slice_in_dim(w_up, at, shar...]
    all_gather x1, waiting for transfers between devices: 10.6 us -> 0.01 us  [local(): gate_piece = lax.all_gather(gate_grad, 'tensor', axis=2, tiled=True)]
    ppermute x0 -> x3, waiting for transfers between devices: none -> 5.86 us  [product_in_turn(): coming = lax.ppermute(carried, axis, ahead) if step < devices - 1 else None]
    unnamed x20 -> x16, local copies, waits for them, and re-layouts: 13.9 us -> 13.2 us
    unnamed x5 -> x4, waiting for transfers between devices: 28.6 us -> 28.1 us
  transfers between devices with their start and end apart: 8 -> 10, of which waited for: 6 -> 5; matrix products, arithmetic and copies ran while one was open for 37% -> 41% of each run, Pallas kernels for 0% -> 0%
where the time goes in v1:
time: 317 us; the launch traced here: 316 us
  waiting for transfers between devices  134 us (42%)
  matrix products  113 us (36%)
  starting transfers between devices  22.4 us (7%)
  local copies, waits for them, and re-layouts  20.6 us (6%)
  between operations  14 us (4%)
  other arithmetic  11.6 us (4%)
    psum x1, waiting for transfers between devices, local(): lax.psum(pre_gate.astype(jnp.bfloat16), 'tensor').astype(jnp.float32)  66 us
    unnamed x4, waiting for transfers between devices  28.1 us
    dot_general x4, matrix products, local(): jnp.einsum('erf,edf->erd', shard, lax.dynamic_slice_in_dim(w_up, at, shar...  26.1 us
    all_to_all x1, waiting for transfers between devices, local(): lax.all_to_all(token_send, 'expert', split_axis=0, concat_axis=1, tiled=T...  24.5 us
    dot_general x1, matrix products, local(): jnp.einsum('erf,erd->efd', hidden, grad_rows, preferred_element_type=jnp....  13.8 us
    dot_general x1, matrix products, local(): jnp.einsum('erf,edf->erd', gate_piece, w_gate, preferred_element_type=jnp...  13.8 us
    dot_general x1, matrix products, local(): jnp.einsum('erd,edf->erf', token_rows, w_up, preferred_element_type=jnp.f...  13.7 us
    dot_general x1, matrix products, local(): jnp.einsum('erd,edf->erf', token_rows, w_gate, preferred_element_type=jnp...  13.7 us
  transfers between devices with their start and end apart: 10, of which 5 were waited for; matrix products, arithmetic and copies ran while one was open for 41% of the time, Pallas kernels for 0%

profile of v1, /device:TPU:0, one launch (start us, length us, event | category | flops | bytes accessed | tf_op | source)
XLA Modules:
  0.0 316.2 jit_solution(13644415257099127169)
XLA Ops:
  7.2 0.0 copy-start
  7.2 0.0 copy-start.4
  7.2 0.8 copy.45
  8.0 0.1 eq.48
  8.1 0.1 eq.44
  8.2 0.8 copy.49
  8.9 0.6 reduce-window.6
  9.6 0.2 slice_reduce_fusion
  9.8 0.1 fusion.27
  9.9 0.1 reduce_sum.30
  10.0 0.4 convert_reduce_fusion
  10.4 0.0 copy-done
  10.4 1.4 fusion.10
  11.8 6.4 %all-to-all-start = ((bf16[64,8,1024]{2,1,0:T(8,128)(2,1)}), bf16[64,8,1024]{2,1,0:T(8,128)(2,1)S(1)}, u32[]{:S(2)}, u32[]{:S(2)}) async-start(bf16[64,8,1024]{2,1,0:T(8,128)(2,1)} %fusion.10), calls=%async_computation | async-start | bytes 2097152 | tf_op jit(solution)/shard_map/all_to_all | solution.py:48
  18.2 0.0 copy-done.4
  18.2 2.1 fusion.11
  20.3 24.5 %all-to-all-done = bf16[64,8,1024]{2,1,0:T(8,128)(2,1)S(1)} async-done(((bf16[64,8,1024]{2,1,0:T(8,128)(2,1)}), bf16[64,8,1024]{2,1,0:T(8,128)(2,1)S(1)}, u32[]{:S(2)}, u32[]{:S(2)}) %all-to-all-start) | async-done | bytes 1048608 | tf_op jit(solution)/shard_map/all_to_all | solution.py:48
  44.8 3.6 %all-to-all-start.2 = ((bf16[64,8,1024]{2,1,0:T(8,128)(2,1)}), bf16[64,8,1024]{2,1,0:T(8,128)(2,1)S(1)}, u32[]{:S(2)}, u32[]{:S(2)}) async-start(bf16[64,8,1024]{2,1,0:T(8,128)(2,1)} %fusion.11), calls=%async_computation.2 | async-start | bytes 2097152 | tf_op jit(solution)/shard_map/all_to_all | solution.py:49
  48.3 0.0 all-reduce.3.cloned.1.call-start
  48.4 13.7 %convolution_convert_fusion.2 = bf16[8,64,1536]{2,1,0:T(8,128)(2,1)} fusion(bf16[8,1024,1536]{2,1,0:T(8,128)(2,1)} %param.12, bf16[8,8,8,1024]{3,2,1,0:T(8,128)(2,1)S(1)} %bitcast.70), kind=kOutput, calls=%fused_computation.12 | convolution fusion | flops 1611399168 | bytes 27787264 | tf_op jit(solution)/shard_map/erd,edf->erf/dot_general | solution.py:52
  62.1 13.7 %convolution_convert_fusion.3 = bf16[8,64,1536]{2,1,0:T(8,128)(2,1)} fusion(bf16[8,1024,1536]{2,1,0:T(8,128)(2,1)} %param.11, bf16[8,8,8,1024]{3,2,1,0:T(8,128)(2,1)S(1)} %bitcast.71), kind=kOutput, calls=%fused_computation.13 | convolution fusion | flops 1611399168 | bytes 27787264 | tf_op jit(solution)/shard_map/erd,edf->erf/dot_general | solution.py:51
  75.7 0.0 all-reduce.3.cloned.1.call-update
  75.8 0.0 reduce-scatter.4.cloned.1.call-start
  75.8 0.0 all-to-all-done.2
  75.8 13.2 %convolution_convert_fusion.1 = bf16[8,64,1536]{2,1,0:T(8,128)(2,1)S(1)} fusion(bf16[8,1536,1024]{2,1,0:T(8,128)(2,1)} %param.13, bf16[8,8,8,1024]{3,2,1,0:T(8,128)(2,1)S(1)} %bitcast.67), kind=kOutput, calls=%fused_computation.11 | convolution fusion | flops 1611399168 | bytes 27787264 | tf_op jit(solution)/shard_map/erd,efd->erf/dot_general | solution.py:68
  89.1 3.5 %copy.60 = bf16[8,64,1536]{1,0,2:T(8,128)(2,1)} copy(bf16[8,64,1536]{2,1,0:T(8,128)(2,1)S(1)} %convolution_convert_fusion.1) | data formatting | bytes 3145728
  92.5 5.4 %reshape.61 = bf16[1536,512]{1,0:T(8,128)(2,1)} reshape(bf16[1536,8,64]{2,1,0:T(8,128)(2,1)} %bitcast.69) | data formatting | bytes 3145728
  98.0 0.0 reduce-scatter.4.cloned.1.call-update
  98.0 0.2 all-gather.2.cloned.1.call-start
  98.3 66.0 %all-reduce.3.cloned.1.call-done = (bf16[8,64,1536]{2,1,0:T(8,128)(2,1)}, bf16[8,64,1536]{2,1,0:T(8,128)(2,1)}) async-done(((bf16[8,64,1536]{2,1,0:T(8,128)(2,1)}, bf16[8,64,1536]{2,1,0:T(8,128)(2,1)}), (bf16[8,64,1536]{2,1,0:T(8,128)(2,1)}, bf16[8,64,1536]{2,1,0:T(8,128)(2,1)})) %all-reduce.3.cloned.1.call-update) | async-done | bytes 3145744 | tf_op jit(solution)/shard_map/psum | solution.py:55
  164.3 3.6 %convert_element_type.70 = f32[8,64,1536]{2,1,0:T(8,128)} convert(bf16[8,64,1536]{2,1,0:T(8,128)(2,1)} %get-tuple-element.5) | non-fusion elementwise | flops 786432 | bytes 4718592 | tf_op jit(solution)/shard_map/convert_element_type | solution.py:55
  167.9 0.0 copy-done.2
  167.9 2.5 add_divide_fusion
  170.3 28.1 %reduce-scatter.4.cloned.1.call-done = bf16[384,512]{1,0:T(8,128)(2,1)} async-done(((bf16[1536,512]{1,0:T(8,128)(2,1)}), bf16[384,512]{1,0:T(8,128)(2,1)}) %reduce-scatter.4.cloned.1.call-update) | async-done | bytes 393232
  198.4 1.5 reshape.62
  199.9 1.2 copy.61
  201.2 1.8 convert_element_type.72
  203.0 0.0 copy-done.3
  203.0 2.5 fusion.24
  205.5 0.0 all-gather.2.cloned.1.call-update
  205.5 1.5 collective-permute-start
  207.0 13.5 %convolution_convert_fusion.4 = bf16[8,64,1024]{2,1,0:T(8,128)(2,1)S(1)} fusion(bf16[8,1536,1024]{2,1,0:T(8,128)(2,1)} %param.13, bf16[8,64,1536]{2,1,0:T(8,128)(2,1)S(1)} %copy-done.2, bf16[8,64,1536]{2,1,0:T(8,128)(2,1)} %get-tuple-element.6), kind=kOutput, calls=%fused_computation.15 | convolution fusion | flops 1617428480 | bytes 29360128 | tf_op jit(solution)/shard_map/erf,efd->erd/dot_general | solution.py:60
  220.6 1.6 copy.51
  222.1 4.6 %all-to-all-start.1 = ((bf16[8,64,1024]{2,0,1:T(8,128)(2,1)}), bf16[8,64,1024]{2,0,1:T(8,128)(2,1)}, u32[]{:S(2)}, u32[]{:S(2)}) async-start(bf16[8,64,1024]{2,0,1:T(8,128)(2,1)} %copy.51), calls=%async_computation.1 | async-start | bytes 2097152 | tf_op jit(solution)/shard_map/all_to_all | solution.py:91
  226.7 0.0 collective-permute-done
  226.7 1.5 collective-permute-start.1
  228.2 6.2 %fusion.6 = f32[8,64,1024]{2,1,0:T(8,128)} fusion(bf16[8,64,384]{2,1,0:T(8,128)(2,1)S(1)} %get-tuple-element.7, bf16[8,1024,1536]{2,1,0:T(8,128)(2,1)} %param.12, s32[]{:T(128)S(6)} %select_n.38), kind=kOutput, calls=%fused_computation.7 | convolution fusion | flops 402653184 | bytes 8781828 | tf_op jit(solution)/shard_map/erf,edf->erd/dot_general | solution.py:82
  234.4 6.3 %fusion.4 = f32[8,64,1024]{2,1,0:T(8,128)} fusion(bf16[8,64,384]{2,1,0:T(8,128)(2,1)} %collective-permute-done, bf16[8,1024,1536]{2,1,0:T(8,128)(2,1)} %param.12, s32[]{:T(128)S(6)} %select_n.40), kind=kOutput, calls=%fused_computation.5 | convolution fusion | flops 402653184 | bytes 8781828 | tf_op jit(solution)/shard_map/erf,edf->erd/dot_general | solution.py:82
  240.8 5.9 %collective-permute-done.1 = bf16[8,64,384]{2,1,0:T(8,128)(2,1)S(1)} collective-permute-done((bf16[8,64,384]{2,1,0:T(8,128)(2,1)}, bf16[8,64,384]{2,1,0:T(8,128)(2,1)S(1)}, u32[]{:S(2)}, u32[]{:S(2)}) %collective-permute-start.1) | collective-permute-done | bytes 393248 | tf_op jit(solution)/shard_map/ppermute | solution.py:12
  246.6 0.0 collective-permute-start.2
  246.6 6.2 %fusion.2 = f32[8,64,1024]{2,1,0:T(8,128)} fusion(bf16[8,64,384]{2,1,0:T(8,128)(2,1)S(1)} %collective-permute-done.1, bf16[8,1024,1536]{2,1,0:T(8,128)(2,1)} %param.12, s32[]{:T(128)S(6)} %select_n.42), kind=kOutput, calls=%fused_computation.3 | convolution fusion | flops 402653184 | bytes 8781828 | tf_op jit(solution)/shard_map/erf,edf->erd/dot_general | solution.py:82
  252.8 13.8 %fusion.35 = f32[8,64,1024]{2,1,0:T(8,128)} fusion(bf16[8,64,1536]{2,1,0:T(8,128)(2,1)} %all-gather.2.cloned.1.call-done, bf16[8,1024,1536]{2,1,0:T(8,128)(2,1)} %param.11), kind=kOutput, calls=%fused_computation.56 | convolution fusion | flops 1610612736 | bytes 28835840 | tf_op jit(solution)/shard_map/erf,edf->erd/dot_general | solution.py:77
  266.6 0.0 collective-permute-done.2
  266.6 7.4 %add_convert_fusion = bf16[8,64,1024]{2,1,0:T(8,128)(2,1)S(1)} fusion(f32[8,64,1024]{2,1,0:T(8,128)} %fusion.35, f32[8,64,1024]{2,1,0:T(8,128)} %fusion.2, f32[8,64,1024]{2,1,0:T(8,128)} %fusion.6, f32[8,64,1024]{2,1,0:T(8,128)} %fusion.4, bf16[8,64,384]{2,1,0:T(8,128)(2,1)S(1)} %collective-permute-done.2, bf16[8,1024,1536]{2,1,0:T(8,128)(2,1)} %param.12, ...), kind=kOutput, calls=%fused_computation.14 | convolution fusion | flops 405274624 | bytes 16121860 | tf_op jit(solution)/shard_map/erf,edf->erd/dot_general | solution.py:82
  274.0 1.7 copy.55
  275.7 0.0 all-to-all-done.1
  275.7 4.6 %all-to-all-start.3 = ((bf16[8,64,1024]{2,0,1:T(8,128)(2,1)}), bf16[8,64,1024]{2,0,1:T(8,128)(2,1)}, u32[]{:S(2)}, u32[]{:S(2)}) async-start(bf16[8,64,1024]{2,0,1:T(8,128)(2,1)} %copy.55), calls=%async_computation.3 | async-start | bytes 2097152 | tf_op jit(solution)/shard_map/all_to_all | solution.py:92
  280.3 13.8 %convolution_convert_fusion = bf16[8,1536,1024]{2,1,0:T(8,128)(2,1)} fusion(bf16[8,8,8,1024]{3,2,1,0:T(8,128)(2,1)S(1)} %bitcast.68, bf16[8,64,1536]{2,1,0:T(8,128)(2,1)S(1)} %copy-done.2, bf16[8,64,1536]{2,1,0:T(8,128)(2,1)} %get-tuple-element.6), kind=kOutput, calls=%fused_computation | convolution fusion | flops 1629487104 | bytes 29360128 | tf_op jit(solution)/shard_map/erf,erd->efd/dot_general | solution.py:63
  294.1 1.9 copy.53
  295.9 1.2 convolution_convert_fusion.8
  297.2 9.8 %all-to-all-done.3 = bf16[8,64,1024]{2,0,1:T(8,128)(2,1)} async-done(((bf16[8,64,1024]{2,0,1:T(8,128)(2,1)}), bf16[8,64,1024]{2,0,1:T(8,128)(2,1)}, u32[]{:S(2)}, u32[]{:S(2)}) %all-to-all-start.3) | async-done | bytes 1048608 | tf_op jit(solution)/shard_map/all_to_all | solution.py:92
  306.9 1.8 copy.57
  308.8 0.9 convolution_convert_fusion.7
  309.7 0.0 copy-done.1
  (8 shorter events, 0.1 us)
Async XLA Ops:
  7.2 3.2 %copy-start = (bf16[32,1024]{1,0:T(8,128)(2,1)S(1)}, bf16[32,1024]{1,0:T(8,128)(2,1)}, u32[]{:S(2)}) copy-start(bf16[32,1024]{1,0:T(8,128)(2,1)} %param.7) | copy-start | bytes 196612
  7.2 11.0 %copy-start.4 = (bf16[32,1024]{1,0:T(8,128)(2,1)S(1)}, bf16[32,1024]{1,0:T(8,128)(2,1)}, u32[]{:S(2)}) copy-start(bf16[32,1024]{1,0:T(8,128)(2,1)} %param.8) | copy-start | bytes 196612
  11.8 32.9 %all-to-all-start = ((bf16[64,8,1024]{2,1,0:T(8,128)(2,1)}), bf16[64,8,1024]{2,1,0:T(8,128)(2,1)S(1)}, u32[]{:S(2)}, u32[]{:S(2)}) async-start(bf16[64,8,1024]{2,1,0:T(8,128)(2,1)} %fusion.10), calls=%async_computation | async-start | bytes 2097152 | tf_op jit(solution)/shard_map/all_to_all | solution.py:48
  44.8 31.1 %all-to-all-start.2 = ((bf16[64,8,1024]{2,1,0:T(8,128)(2,1)}), bf16[64,8,1024]{2,1,0:T(8,128)(2,1)S(1)}, u32[]{:S(2)}, u32[]{:S(2)}) async-start(bf16[64,8,1024]{2,1,0:T(8,128)(2,1)} %fusion.11), calls=%async_computation.2 | async-start | bytes 2097152 | tf_op jit(solution)/shard_map/all_to_all | solution.py:49
  48.3 115.9 %all-reduce.3.cloned.1.call-start = ((), (), s32[]{:S(2)}) async-start(), calls=%async_computation.7 | async-start | bytes 6291456 | tf_op jit(solution)/shard_map/psum | solution.py:55
  75.8 122.6 %reduce-scatter.4.cloned.1.call-start = ((), (), s32[]{:S(2)}) async-start(), calls=%async_computation.6 | async-start | bytes 1966080
  98.0 154.8 %all-gather.2.cloned.1.call-start = ((), (), s32[]{:S(2)}) async-start(), calls=%async_computation.5 | async-start | bytes 1966080 | tf_op jit(solution)/shard_map/all_gather | solution.py:76
  164.3 3.6 %copy-start.2 = (bf16[8,64,1536]{2,1,0:T(8,128)(2,1)S(1)}, bf16[8,64,1536]{2,1,0:T(8,128)(2,1)}, u32[]{:S(2)}) copy-start(bf16[8,64,1536]{2,1,0:T(8,128)(2,1)} %get-tuple-element.5) | copy-start | bytes 4718596
  201.2 1.9 copy-start.3
  205.5 21.2 %collective-permute-start = (bf16[8,64,384]{2,1,0:T(8,128)(2,1)S(1)}, bf16[8,64,384]{2,1,0:T(8,128)(2,1)}, u32[]{:S(2)}, u32[]{:S(2)}) collective-permute-start(bf16[8,64,384]{2,1,0:T(8,128)(2,1)S(1)} %get-tuple-element.7), channel_id=1, source_target_pairs={{0,1},{1,2},{2,3},{3,0},{4,5},{5,6},{6,7},{7,4},{8,9},{9,10},{10,1... | collective-permute-start | bytes 1179656 | tf_op jit(solution)/shard_map/ppermute | solution.py:12
  222.1 53.5 %all-to-all-start.1 = ((bf16[8,64,1024]{2,0,1:T(8,128)(2,1)}), bf16[8,64,1024]{2,0,1:T(8,128)(2,1)}, u32[]{:S(2)}, u32[]{:S(2)}) async-start(bf16[8,64,1024]{2,0,1:T(8,128)(2,1)} %copy.51), calls=%async_computation.1 | async-start | bytes 2097152 | tf_op jit(solution)/shard_map/all_to_all | solution.py:91
  226.7 19.9 %collective-permute-start.1 = (bf16[8,64,384]{2,1,0:T(8,128)(2,1)}, bf16[8,64,384]{2,1,0:T(8,128)(2,1)S(1)}, u32[]{:S(2)}, u32[]{:S(2)}) collective-permute-start(bf16[8,64,384]{2,1,0:T(8,128)(2,1)} %collective-permute-done), channel_id=1, source_target_pairs={{0,1},{1,2},{2,3},{3,0},{4,5},{5,6},{6,7},{7,4},{8,9},{9,10},{10,1... | collective-permute-start | bytes 1179656 | tf_op jit(solution)/shard_map/ppermute | solution.py:12
  246.6 20.0 %collective-permute-start.2 = (bf16[8,64,384]{2,1,0:T(8,128)(2,1)S(1)}, bf16[8,64,384]{2,1,0:T(8,128)(2,1)S(1)}, u32[]{:S(2)}, u32[]{:S(2)}) collective-permute-start(bf16[8,64,384]{2,1,0:T(8,128)(2,1)S(1)} %collective-permute-done.1), channel_id=1, source_target_pairs={{0,1},{1,2},{2,3},{3,0},{4,5},{5,6},{6,7},{7,4},{8,9},{9,10},{10,1... | collective-permute-start | bytes 1179656 | tf_op jit(solution)/shard_map/ppermute | solution.py:12
  275.7 31.3 %all-to-all-start.3 = ((bf16[8,64,1024]{2,0,1:T(8,128)(2,1)}), bf16[8,64,1024]{2,0,1:T(8,128)(2,1)}, u32[]{:S(2)}, u32[]{:S(2)}) async-start(bf16[8,64,1024]{2,0,1:T(8,128)(2,1)} %copy.55), calls=%async_computation.3 | async-start | bytes 2097152 | tf_op jit(solution)/shard_map/all_to_all | solution.py:92
  294.1 15.6 %copy-start.1 = (bf16[32,1024]{1,0:T(8,128)(2,1)S(1)}, bf16[32,1024]{1,0:T(8,128)(2,1)}, u32[]{:S(2)}) copy-start(bf16[32,1024]{1,0:T(8,128)(2,1)} %param.7) | copy-start | bytes 196612
Sparse Core Ops, SparseCore 0:
  75.9 88.3 all-reduce.2
  167.2 31.1 reduce-scatter.3
  205.6 39.3 all-gather.1
